TPU v7x, 512 devices: a whole 4x4x16 slice. The times are simulated.
512 devices in a mesh: sub: 8 (over z_hi, y), rng: 64 (over z_lo, x, core).
Axes of the slice: x: 4, y: 4, z: 16 (z_hi: 2, z_lo: 8; z = z_hi * 8 + z_lo), core: 2. Of those that a mesh axis runs over, the one named last changes fastest.
Arguments:
- echoes: bfloat16 [2, 4096, 32768], P(None, ('sub', 'rng')), may hold values from -6 to 6
- fore_flag: int32 [3, 8, 64], P(None, None, 'rng'), may hold values from 0 to 1, as said below
- band_offset: int32 [3, 8, 64], P(None, None, 'rng'), may hold values from -16 to 16, as said below
- angle_interp: bfloat16 [3, 2, 512, 256], replicated, may hold values from -1 to 1
- range_kernel: bfloat16 [3, 544, 512], replicated, may hold values from -1 to 2, as said below
- center_shift: float32 [3, 8], replicated, may hold values from -6 to 6
Outputs:
- focused_image: float32 [2, 4096, 32768], P(None, 'sub', 'rng')
Inputs may be any that keep to these rules, and one draw needn't show every extreme that they name: fore_flag[l, g, b] + fore_flag[l, g XOR 2**l, b] = 1 for every level l, group g and block b. `band_offset`: in every level both -16 and 16 occur. range_kernel[l, w, r] = 0 wherever |w - 16 - r| > 16.
All inputs are finite; a program needn't handle non-finite values.
Results may differ from a plain program's by a relative error of at most 0.0076.
Values may be sent and summed in bfloat16 or wider, within the bound.
A program may use at most 64 MiB of HBM per device.

v0:
```python
import math

import jax
import jax.numpy as jnp
from jax import lax
from jax.sharding import PartitionSpec as P

ANGLES = 512
PULSES = 512
BAND_HALF = 16
RIM_WIDTH = 32


def padded(value, sides, width):
    for axis, dim in sides:
        devices, length = (lax.axis_size(axis), value.shape[dim])
        up = [(i, (i + 1) % devices) for i in range(devices - 1)]
        down = [(j, i) for i, j in up]
        last = lax.slice_in_dim(value, length - width, length, axis=dim)
        leading = lax.slice_in_dim(value, 0, width, axis=dim)
        before = lax.ppermute(last, axis, up)
        after = lax.ppermute(leading, axis, down)
        value = jnp.concatenate([before, value, after], axis=dim)
    return value


def from_partner(value, axis, apart):
    mask = 2**apart
    pairs = [(source, source ^ mask) for source in range(lax.axis_size(axis))]
    return lax.ppermute(value, axis, pairs)


def doppler_matrix(angles, pulses):
    angle_ids = jnp.arange(angles, dtype=jnp.int32)[:, None]
    pulse_ids = jnp.arange(pulses, dtype=jnp.int32)[None, :]
    cycles = (2 * angle_ids + 1 - angles) * pulse_ids % (2 * angles)
    phase_angle = math.pi / angles * cycles.astype(jnp.float32)
    cosine = jnp.cos(phase_angle) / math.sqrt(pulses)
    sine_part = jnp.sin(phase_angle) / math.sqrt(pulses)
    upper_rows = jnp.concatenate([cosine, sine_part], axis=1)
    bottom = jnp.concatenate([-sine_part, cosine], axis=1)
    return jnp.concatenate([upper_rows, bottom], axis=0).astype(jnp.bfloat16)


def phase_turn(real_imag, shift_rate, block_start, total_bins):
    angles = real_imag.shape[1]
    bin_count = real_imag.shape[2]
    angle_pos = (jnp.arange(angles).astype(jnp.float32)[:, None] + 0.5) / angles - 0.5
    range_pos = (
        1.0 + (block_start + jnp.arange(bin_count)).astype(jnp.float32)[None, :] / total_bins
    )
    phase_angle = math.pi * shift_rate * angle_pos * range_pos
    cosine = jnp.cos(phase_angle)
    sine_part = jnp.sin(phase_angle)
    real_part = real_imag[0] * cosine - real_imag[1] * sine_part
    imag_part = real_imag[0] * sine_part + real_imag[1] * cosine
    return jnp.stack([real_part, imag_part])


def on_device(echoes, fore_flag, band_offset, angle_interp, range_kernel, center_shift):
    group_index = lax.axis_index("sub")
    block_index = lax.axis_index("rng")
    sub_count = lax.axis_size("sub")
    rng_count = lax.axis_size("rng")
    local_pulses = echoes.shape[1]
    block_bins = echoes.shape[2] // rng_count
    total_bins = block_bins * rng_count
    block_start = block_index * block_bins
    filter_matrix = doppler_matrix(ANGLES, PULSES)
    split_echoes = echoes.reshape(2, local_pulses, rng_count, block_bins)
    doppler_received = lax.all_to_all(split_echoes, "rng", split_axis=2, concat_axis=1, tiled=True)
    columns = doppler_received.shape[3]
    stacked = doppler_received.reshape(2 * PULSES, columns)
    filtered = jnp.dot(filter_matrix, stacked, preferred_element_type=jnp.float32)
    sector_image = filtered.astype(jnp.bfloat16).reshape(2, ANGLES, columns)
    levels = min(3, sub_count // 2)
    half_rows = ANGLES // 2
    group_ids = jnp.arange(sub_count, dtype=jnp.int32)
    for tree_level in range(levels):
        stride = 2**tree_level
        upper_side = group_index // stride % 2
        partner = group_index + (1 - 2 * upper_side) * stride
        own_mask = group_ids == group_index
        partner_mask = group_ids == partner
        own_flag = jnp.sum(jnp.where(own_mask, fore_flag[tree_level, :, 0], 0))
        partner_flag = 1 - own_flag
        own_shift = jnp.sum(jnp.where(own_mask, center_shift[tree_level], 0.0))
        partner_shift = jnp.sum(jnp.where(partner_mask, center_shift[tree_level], 0.0))
        offset = jnp.sum(jnp.where(own_mask, band_offset[tree_level, :, 0], 0))
        extended = padded(sector_image, (("rng", 2),), RIM_WIDTH)
        window = lax.dynamic_slice_in_dim(
            extended, RIM_WIDTH - BAND_HALF + offset, block_bins + 2 * BAND_HALF, 2
        )
        resampled = jnp.einsum(
            "caw,wr->car", window, range_kernel[tree_level], preferred_element_type=jnp.float32
        ).astype(jnp.bfloat16)
        own_rows = lax.dynamic_slice_in_dim(resampled, own_flag * half_rows, half_rows, 1)
        received = from_partner(resampled, "sub", tree_level)
        partner_rows = lax.dynamic_slice_in_dim(received, own_flag * half_rows, half_rows, 1)
        own_matrix = lax.dynamic_index_in_dim(angle_interp[tree_level], own_flag, 0, keepdims=False)
        partner_matrix = lax.dynamic_index_in_dim(
            angle_interp[tree_level], partner_flag, 0, keepdims=False
        )
        own_term = jnp.einsum(
            "pa,car->cpr", own_matrix, own_rows, preferred_element_type=jnp.float32
        )
        partner_term = jnp.einsum(
            "pa,car->cpr", partner_matrix, partner_rows, preferred_element_type=jnp.float32
        )
        merged = phase_turn(own_term, own_shift, block_start, total_bins)
        merged = merged + phase_turn(partner_term, partner_shift, block_start, total_bins)
        if tree_level + 1 < levels:
            sector_image = merged.astype(jnp.bfloat16)
        else:
            sector_image = merged
    return sector_image


def solution(mesh):
    placed = (
        P(None, ("sub", "rng"), None),
        P(None, None, "rng"),
        P(None, None, "rng"),
        P(),
        P(),
        P(),
    )
    return jax.shard_map(
        on_device, mesh=mesh, in_specs=placed, out_specs=P(None, "sub", "rng"), check_vma=False
    )
```

profile of v0, /device:TPU:31, one launch (start us, length us, event | category | flops | bytes accessed | tf_op | source)
XLA Modules:
  0.0 294.0 jit_solution(10799815896149723771)
XLA Ops:
  0.0 2.3 copy.47
  2.3 16.3 %all-to-all-start = ((bf16[2,8,64,512]{3,1,0,2:T(8,128)(2,1)}), bf16[2,8,64,512]{3,1,0,2:T(8,128)(2,1)S(1)}, u32[]{:S(2)}, u32[]{:S(2)}) async-start(bf16[2,8,64,512]{3,1,0,2:T(8,128)(2,1)} %bitcast.103), calls=%async_computation | async-start | bytes 2097152 | tf_op jit(solution)/shard_map/all_to_all | solution.py:71
  18.7 5.6 %fusion.64 = (bf16[512,512]{1,0:T(8,128)(2,1)S(1)}, bf16[512,512]{1,0:T(8,128)(2,1)S(1)}, bf16[512,512]{1,0:T(8,128)(2,1)}) fusion(s32[512]{0:T(512)S(1)} %multiply_add_fusion.2), kind=kLoop, calls=%fused_computation.99 | loop fusion | flops 5242880 | bytes 1574912 | tf_op jit(solution)/shard_map/convert.5
  24.3 44.8 %all-to-all-done = bf16[2,8,64,512]{3,1,0,2:T(8,128)(2,1)S(1)} async-done(((bf16[2,8,64,512]{3,1,0,2:T(8,128)(2,1)}), bf16[2,8,64,512]{3,1,0,2:T(8,128)(2,1)S(1)}, u32[]{:S(2)}, u32[]{:S(2)}) %all-to-all-start) | async-done | bytes 1048608 | tf_op jit(solution)/shard_map/all_to_all | solution.py:71
  69.1 1.0 copy-done.1
  70.1 1.2 fusion.10
  71.9 1.9 collective-permute-start
  73.9 3.2 %collective-permute-start.1 = (bf16[2,512,32]{1,2,0:T(8,128)(2,1)S(1)}, bf16[2,512,32]{1,2,0:T(8,128)(2,1)S(1)}, u32[]{:S(2)}, u32[]{:S(2)}) collective-permute-start(bf16[2,512,32]{1,2,0:T(8,128)(2,1)S(1)} %get-tuple-element.36), channel_id=1, source_target_pairs={{1,0},{2,1},{3,2},{4,3},{5,4},{6,5},{7,6},{8,7},{9,8},{10,9},{11,1... | collective-permute-start | bytes 196616 | tf_op jit(solution)/shard_map/ppermute | solution.py:22
  77.1 0.7 fusion.108
  79.1 2.4 collective-permute-done.1
  81.6 3.4 %convolution_convert_fusion.2 = bf16[2,512,512]{2,1,0:T(8,128)(2,1)} fusion(s32[]{:T(128)S(6)} %select_n.115, bf16[2,512,32]{1,2,0:T(8,128)(2,1)S(1)} %collective-permute-done, bf16[2,512,512]{1,2,0:T(8,128)(2,1)S(1)} %copy.29, bf16[2,512,32]{1,2,0:T(8,128)(2,1)S(1)} %collective-permute-done.1, bf16[3,544,512]{2,1,0:T(8,128)(2,1)} %param.10), kind=kOutput, calls=%fused_computation.37 | convolution fusion | flops 574291968 | bytes 2785284 | tf_op jit(solution)/shard_map/caw,wr->car/dot_general | solution.py:94
  84.9 2.4 collective-permute-start.2
  90.2 0.7 fusion.106
  92.9 1.5 convolution_bitcast_fusion.5
  94.4 17.7 %collective-permute-done.2 = bf16[2,512,512]{2,1,0:T(8,128)(2,1)} collective-permute-done((bf16[2,512,512]{2,1,0:T(8,128)(2,1)}, bf16[2,512,512]{2,1,0:T(8,128)(2,1)}, u32[]{:S(2)}, u32[]{:S(2)}) %collective-permute-start.2) | collective-permute-done | bytes 1048608 | tf_op jit(solution)/shard_map/ppermute | solution.py:30
  112.1 1.5 convolution_bitcast_fusion.4
  113.6 8.0 %fusion.54 = (f32[1,512,512]{1,2,0:T(8,128)S(1)}, f32[1,512,512]{1,2,0:T(8,128)S(1)}, f32[1,512,512]{1,2,0:T(8,128)S(1)}, f32[1,512,512]{1,2,0:T(8,128)S(1)}) fusion(f32[2,512,512]{1,2,0:T(8,128)S(1)} %convolution_bitcast_fusion.4, f32[512]{0:T(512)S(1)} %get-tuple-element.51, f32[512]{0:T(512)S(1)} %get-tuple-element.50, ...), kind=kLoop, calls=%fused_computation.85 | loop fusion | flops 3670016 | bytes 8394752 | tf_op jit(solution)/shard_map/sub | solution.py:55
  122.2 1.9 collective-permute-start.3
  124.2 2.4 collective-permute-start.4
  127.8 4.0 %collective-permute-done.4 = bf16[2,512,32]{1,2,0:T(8,128)(2,1)S(1)} collective-permute-done((bf16[2,512,32]{1,2,0:T(8,128)(2,1)S(1)}, bf16[2,512,32]{1,2,0:T(8,128)(2,1)S(1)}, u32[]{:S(2)}, u32[]{:S(2)}) %collective-permute-start.4) | collective-permute-done | bytes 65568 | tf_op jit(solution)/shard_map/ppermute | solution.py:22
  131.9 2.4 convolution_convert_fusion.1
  134.2 3.1 %collective-permute-start.5 = (bf16[2,512,512]{2,1,0:T(8,128)(2,1)S(1)}, bf16[2,512,512]{2,1,0:T(8,128)(2,1)S(1)}, u32[]{:S(2)}, u32[]{:S(2)}) collective-permute-start(bf16[2,512,512]{2,1,0:T(8,128)(2,1)S(1)} %convolution_convert_fusion.1), channel_id=1, source_target_pairs={{0,128},{64,192},{128,0},{192,64},{256,384},{320,448},{384,256},{4... | collective-permute-start | bytes 3145736 | tf_op jit(solution)/shard_map/ppermute | solution.py:30
  142.4 18.8 %collective-permute-done.5 = bf16[2,512,512]{2,1,0:T(8,128)(2,1)S(1)} collective-permute-done((bf16[2,512,512]{2,1,0:T(8,128)(2,1)S(1)}, bf16[2,512,512]{2,1,0:T(8,128)(2,1)S(1)}, u32[]{:S(2)}, u32[]{:S(2)}) %collective-permute-start.5) | collective-permute-done | bytes 1048608 | tf_op jit(solution)/shard_map/ppermute | solution.py:30
  161.7 8.0 %fusion.50 = (f32[1,512,512]{1,2,0:T(8,128)S(1)}, f32[1,512,512]{1,2,0:T(8,128)S(1)}, f32[1,512,512]{1,2,0:T(8,128)S(1)}, f32[1,512,512]{1,2,0:T(8,128)S(1)}) fusion(f32[2,512,512]{1,2,0:T(8,128)S(1)} %convolution_bitcast_fusion.2, f32[512]{0:T(512)S(1)} %get-tuple-element.52, f32[512]{0:T(512)S(1)} %get-tuple-element.50, ...), kind=kLoop, calls=%fused_computation.81 | loop fusion | flops 3670016 | bytes 8394752 | tf_op jit(solution)/shard_map/sub | solution.py:55
  170.3 1.9 collective-permute-start.6
  172.3 2.4 collective-permute-start.7
  175.9 4.0 %collective-permute-done.7 = bf16[2,512,32]{1,2,0:T(8,128)(2,1)S(1)} collective-permute-done((bf16[2,512,32]{1,2,0:T(8,128)(2,1)S(1)}, bf16[2,512,32]{1,2,0:T(8,128)(2,1)S(1)}, u32[]{:S(2)}, u32[]{:S(2)}) %collective-permute-start.7) | collective-permute-done | bytes 65568 | tf_op jit(solution)/shard_map/ppermute | solution.py:22
  179.9 2.4 convolution_convert_fusion
  182.4 8.0 %collective-permute-start.8 = (bf16[2,512,512]{2,1,0:T(8,128)(2,1)S(1)}, bf16[2,512,512]{2,1,0:T(8,128)(2,1)S(1)}, u32[]{:S(2)}, u32[]{:S(2)}) collective-permute-start(bf16[2,512,512]{2,1,0:T(8,128)(2,1)S(1)} %convolution_convert_fusion), channel_id=1, source_target_pairs={{0,256},{64,320},{128,384},{192,448},{256,0},{320,64},{384,128},{4... | collective-permute-start | bytes 3145736 | tf_op jit(solution)/shard_map/ppermute | solution.py:30
  196.3 86.9 %collective-permute-done.8 = bf16[2,512,512]{2,1,0:T(8,128)(2,1)S(1)} collective-permute-done((bf16[2,512,512]{2,1,0:T(8,128)(2,1)S(1)}, bf16[2,512,512]{2,1,0:T(8,128)(2,1)S(1)}, u32[]{:S(2)}, u32[]{:S(2)}) %collective-permute-start.8) | collective-permute-done | bytes 1048608 | tf_op jit(solution)/shard_map/ppermute | solution.py:30
  283.6 8.0 %fusion.46 = (f32[1,512,512]{1,2,0:T(8,128)S(1)}, f32[1,512,512]{1,2,0:T(8,128)S(1)}, f32[1,512,512]{1,2,0:T(8,128)S(1)}, f32[1,512,512]{1,2,0:T(8,128)S(1)}) fusion(f32[2,512,512]{1,2,0:T(8,128)S(1)} %convolution_bitcast_fusion, f32[512]{0:T(512)S(1)} %get-tuple-element.54, f32[512]{0:T(512)S(1)} %get-tuple-element.50, ...), kind=kLoop, calls=%fused_computation.77 | loop fusion | flops 3670016 | bytes 8394752 | tf_op jit(solution)/shard_map/sub | solution.py:55
  292.2 1.8 copy.38
  (30 shorter events, 4.4 us)
Async XLA Ops:
  2.3 66.7 %all-to-all-start = ((bf16[2,8,64,512]{3,1,0,2:T(8,128)(2,1)}), bf16[2,8,64,512]{3,1,0,2:T(8,128)(2,1)S(1)}, u32[]{:S(2)}, u32[]{:S(2)}) async-start(bf16[2,8,64,512]{3,1,0,2:T(8,128)(2,1)} %bitcast.103), calls=%async_computation | async-start | bytes 2097152 | tf_op jit(solution)/shard_map/all_to_all | solution.py:71
  69.1 1.0 copy-start.1
  71.3 5.7 %copy-start.2 = (s32[3,8,1]{1,2,0:T(1,128)S(1)}, s32[3,8,1]{1,2,0:T(1,128)}, u32[]{:S(2)}) copy-start(s32[3,8,1]{1,2,0:T(1,128)} %param.7) | copy-start | bytes 292
  71.4 5.7 %copy-start.3 = (s32[3,8,1]{1,2,0:T(1,128)S(1)}, s32[3,8,1]{1,2,0:T(1,128)}, u32[]{:S(2)}) copy-start(s32[3,8,1]{1,2,0:T(1,128)} %param.8) | copy-start | bytes 292
  71.9 7.2 %collective-permute-start = (bf16[2,512,32]{1,2,0:T(8,128)(2,1)S(1)}, bf16[2,512,32]{1,2,0:T(8,128)(2,1)S(1)}, u32[]{:S(2)}, u32[]{:S(2)}) collective-permute-start(bf16[2,512,32]{1,2,0:T(8,128)(2,1)S(1)} %get-tuple-element.37), channel_id=1, source_target_pairs={{0,1},{1,2},{2,3},{3,4},{4,5},{5,6},{6,7},{7,8},{8,9},{9,10},{10,1... | collective-permute-start | bytes 196616 | tf_op jit(solution)/shard_map/ppermute | solution.py:21
  73.9 7.7 %collective-permute-start.1 = (bf16[2,512,32]{1,2,0:T(8,128)(2,1)S(1)}, bf16[2,512,32]{1,2,0:T(8,128)(2,1)S(1)}, u32[]{:S(2)}, u32[]{:S(2)}) collective-permute-start(bf16[2,512,32]{1,2,0:T(8,128)(2,1)S(1)} %get-tuple-element.36), channel_id=1, source_target_pairs={{1,0},{2,1},{3,2},{4,3},{5,4},{6,5},{7,6},{8,7},{9,8},{10,9},{11,1... | collective-permute-start | bytes 196616 | tf_op jit(solution)/shard_map/ppermute | solution.py:22
  79.1 11.1 %copy-start.4 = (f32[3,8]{1,0:T(4,128)S(1)}, f32[3,8]{1,0:T(4,128)}, u32[]{:S(2)}) copy-start(f32[3,8]{1,0:T(4,128)} %param.11) | copy-start | bytes 292
  79.1 13.6 %copy-start = (bf16[3,2,512,256]{3,2,1,0:T(8,128)(2,1)S(1)}, bf16[3,2,512,256]{3,2,1,0:T(8,128)(2,1)}, u32[]{:S(2)}) copy-start(bf16[3,2,512,256]{3,2,1,0:T(8,128)(2,1)} %param.9) | copy-start | bytes 4718596
  84.9 27.2 %collective-permute-start.2 = (bf16[2,512,512]{2,1,0:T(8,128)(2,1)}, bf16[2,512,512]{2,1,0:T(8,128)(2,1)}, u32[]{:S(2)}, u32[]{:S(2)}) collective-permute-start(bf16[2,512,512]{2,1,0:T(8,128)(2,1)} %convolution_convert_fusion.2), channel_id=1, source_target_pairs={{0,64},{64,0},{128,192},{192,128},{256,320},{320,256},{384,448},{4... | collective-permute-start | bytes 3145736 | tf_op jit(solution)/shard_map/ppermute | solution.py:30
  122.2 5.6 %collective-permute-start.3 = (bf16[2,512,32]{1,2,0:T(8,128)(2,1)S(1)}, bf16[2,512,32]{1,2,0:T(8,128)(2,1)S(1)}, u32[]{:S(2)}, u32[]{:S(2)}) collective-permute-start(bf16[2,512,32]{1,2,0:T(8,128)(2,1)S(1)} %get-tuple-element.35), channel_id=1, source_target_pairs={{0,1},{1,2},{2,3},{3,4},{4,5},{5,6},{6,7},{7,8},{8,9},{9,10},{10,1... | collective-permute-start | bytes 196616 | tf_op jit(solution)/shard_map/ppermute | solution.py:21
  124.2 7.7 %collective-permute-start.4 = (bf16[2,512,32]{1,2,0:T(8,128)(2,1)S(1)}, bf16[2,512,32]{1,2,0:T(8,128)(2,1)S(1)}, u32[]{:S(2)}, u32[]{:S(2)}) collective-permute-start(bf16[2,512,32]{1,2,0:T(8,128)(2,1)S(1)} %get-tuple-element.34), channel_id=1, source_target_pairs={{1,0},{2,1},{3,2},{4,3},{5,4},{6,5},{7,6},{8,7},{9,8},{10,9},{11,1... | collective-permute-start | bytes 196616 | tf_op jit(solution)/shard_map/ppermute | solution.py:22
  134.2 27.0 %collective-permute-start.5 = (bf16[2,512,512]{2,1,0:T(8,128)(2,1)S(1)}, bf16[2,512,512]{2,1,0:T(8,128)(2,1)S(1)}, u32[]{:S(2)}, u32[]{:S(2)}) collective-permute-start(bf16[2,512,512]{2,1,0:T(8,128)(2,1)S(1)} %convolution_convert_fusion.1), channel_id=1, source_target_pairs={{0,128},{64,192},{128,0},{192,64},{256,384},{320,448},{384,256},{4... | collective-permute-start | bytes 3145736 | tf_op jit(solution)/shard_map/ppermute | solution.py:30
  170.3 5.6 %collective-permute-start.6 = (bf16[2,512,32]{1,2,0:T(8,128)(2,1)S(1)}, bf16[2,512,32]{1,2,0:T(8,128)(2,1)S(1)}, u32[]{:S(2)}, u32[]{:S(2)}) collective-permute-start(bf16[2,512,32]{1,2,0:T(8,128)(2,1)S(1)} %get-tuple-element.33), channel_id=1, source_target_pairs={{0,1},{1,2},{2,3},{3,4},{4,5},{5,6},{6,7},{7,8},{8,9},{9,10},{10,1... | collective-permute-start | bytes 196616 | tf_op jit(solution)/shard_map/ppermute | solution.py:21
  172.3 7.7 %collective-permute-start.7 = (bf16[2,512,32]{1,2,0:T(8,128)(2,1)S(1)}, bf16[2,512,32]{1,2,0:T(8,128)(2,1)S(1)}, u32[]{:S(2)}, u32[]{:S(2)}) collective-permute-start(bf16[2,512,32]{1,2,0:T(8,128)(2,1)S(1)} %get-tuple-element.32), channel_id=1, source_target_pairs={{1,0},{2,1},{3,2},{4,3},{5,4},{6,5},{7,6},{8,7},{9,8},{10,9},{11,1... | collective-permute-start | bytes 196616 | tf_op jit(solution)/shard_map/ppermute | solution.py:22
  182.4 100.8 %collective-permute-start.8 = (bf16[2,512,512]{2,1,0:T(8,128)(2,1)S(1)}, bf16[2,512,512]{2,1,0:T(8,128)(2,1)S(1)}, u32[]{:S(2)}, u32[]{:S(2)}) collective-permute-start(bf16[2,512,512]{2,1,0:T(8,128)(2,1)S(1)} %convolution_convert_fusion), channel_id=1, source_target_pairs={{0,256},{64,320},{128,384},{192,448},{256,0},{320,64},{384,128},{4... | collective-permute-start | bytes 3145736 | tf_op jit(solution)/shard_map/ppermute | solution.py:30
where the time goes:
time: 295 us; the launch traced here: 294 us
  waiting for transfers between devices  179 us (61%)
  starting transfers between devices  43.4 us (15%)
  other arithmetic  32.7 us (11%)
  between operations  19 us (6%)
  matrix products  14.4 us (5%)
  local copies, waits for them, and re-layouts  5.9 us (2%)
    ppermute x3, waiting for transfers between devices, from_partner(): return lax.ppermute(value, axis, pairs)  123 us
    all_to_all x1, waiting for transfers between devices, on_device(): lax.all_to_all(split_echoes, 'rng', split_axis=2, concat_axis=1, tiled=True)  44.8 us
    sub x3, other arithmetic, phase_turn(): real_part = real_imag[0] * cosine - real_imag[1] * sine_part  24.1 us
    all_to_all x1, starting transfers between devices, on_device(): lax.all_to_all(split_echoes, 'rng', split_axis=2, concat_axis=1, tiled=True)  16.3 us
    ppermute x3, starting transfers between devices, from_partner(): return lax.ppermute(value, axis, pairs)  13.4 us
    ppermute x3, waiting for transfers between devices, padded(): after = lax.ppermute(leading, axis, down)  10.4 us
    dot_general x3, matrix products, on_device(): jnp.einsum('caw,wr->car', window, range_kernel[tree_level], preferred_ele...  8.15 us
    ppermute x3, starting transfers between devices, padded(): after = lax.ppermute(leading, axis, down)  7.98 us
  transfers between devices with their start and end apart: 10, of which 7 were waited for; matrix products, arithmetic and copies ran while one was open for 3% of the time, Pallas kernels for 0%

commit v1 on v0

v1 whole, which is shorter than its diff:
```python
import functools
import math

import jax
import jax.numpy as jnp
import ml_dtypes
import numpy as np
from jax import lax
from jax.experimental import pallas as pl
from jax.experimental.pallas import tpu as pltpu
from jax.sharding import PartitionSpec as P

ANGLES = 512
PULSES = 512
BINS = 512
TILE = 128
TILES = BINS // TILE
HALF = ANGLES // 2
BAND_HALF = 16
LEVELS = 3
MESH = pl.DeviceIdType.MESH
ORDER = (1, 2, 0, 3)


def doppler_constant(sources):
    angle = np.arange(ANGLES, dtype=np.int64)[:, None]
    pulse = np.arange(PULSES, dtype=np.int64)[None, :]
    cycles = (2 * angle + 1 - ANGLES) * pulse % (2 * ANGLES)
    phase = math.pi / ANGLES * cycles
    cosine = np.cos(phase) / math.sqrt(PULSES)
    sine = np.sin(phase) / math.sqrt(PULSES)
    whole = np.block([[cosine, sine], [-sine, cosine]])
    whole = whole.reshape(2 * ANGLES, 2, sources, PULSES // sources)
    return whole.transpose(0, 2, 1, 3).reshape(2 * ANGLES, 2 * PULSES).astype(ml_dtypes.bfloat16)


def kernel(
    sources,
    total_bins,
    echoes,
    doppler,
    kernels,
    interp,
    flags,
    offsets,
    shifts,
    out,
    turned,
    wide,
    shifted,
    chosen,
    images,
    left_rim,
    right_rim,
    given,
    kept,
    taken,
    total,
    cos_table,
    sin_table,
    turn_sem,
    wide_sem,
    rim_send,
    rim_recv,
    pair_send,
    pair_recv,
    out_sem,
):
    group = lax.axis_index("sub")
    block = lax.axis_index("rng")
    partners = [jnp.bitwise_xor(group, 1 << level) for level in range(LEVELS)]

    barrier = pltpu.get_barrier_semaphore()

    def greet(step, carry):
        peer = lax.rem(block + step, sources)
        pl.semaphore_signal(barrier, inc=1, device_id=(group, peer), device_id_type=MESH)
        return carry

    for partner in partners[::-1]:
        pl.semaphore_signal(barrier, inc=1, device_id=(partner, block), device_id_type=MESH)
    lax.fori_loop(1, sources, greet, 0)
    load = pltpu.make_async_copy(doppler, wide, wide_sem)
    load.start()
    pl.semaphore_wait(barrier, sources - 1 + LEVELS)

    def turn(step, carry):
        peer = lax.rem(block + step, sources)
        pltpu.make_async_remote_copy(
            src_ref=echoes.at[:, pl.ds(pl.multiple_of(peer * BINS, BINS), BINS)],
            dst_ref=turned.at[block],
            send_sem=turn_sem.at[0],
            recv_sem=turn_sem.at[1],
            device_id=(group, peer),
            device_id_type=MESH,
        ).start()
        return carry

    lax.fori_loop(1, sources, turn, 0)
    stay = pltpu.make_async_copy(
        echoes.at[:, pl.ds(pl.multiple_of(block * BINS, BINS), BINS)], turned.at[block], turn_sem.at[2]
    )
    stay.start()

    for level in range(LEVELS):
        offset = offsets[level, group]
        rows = lax.broadcasted_iota(jnp.int32, (TILE, BINS + 2 * BAND_HALF), 0)
        taps = lax.broadcasted_iota(jnp.int32, (TILE, BINS + 2 * BAND_HALF), 1)

        def shift(step, carry, level=level, offset=offset, rows=rows, taps=taps):
            start = pl.multiple_of(step * TILE, TILE)
            pick = jnp.where(rows + start == taps + (TILE - BAND_HALF + offset), 1.0, 0.0).astype(jnp.bfloat16)
            moved = jnp.dot(pick, kernels[level], preferred_element_type=jnp.float32)
            shifted[level, pl.ds(start, TILE), :] = moved.astype(jnp.bfloat16)
            return carry

        lax.fori_loop(0, TILES + 2, shift, 0)

        def choose(step, carry, level=level):
            rows = pl.ds(pl.multiple_of(step * TILE, TILE), TILE)
            zero = interp[level, 0, rows, :].astype(jnp.float32)
            one = interp[level, 1, rows, :].astype(jnp.float32)
            side = jnp.full((TILE, HALF), flags[level, group], jnp.int32)
            chosen[level, 0, rows, :] = jnp.where(side == 1, one, zero).astype(jnp.bfloat16)
            chosen[level, 1, rows, :] = jnp.where(side == 1, zero, one).astype(jnp.bfloat16)
            return carry

        lax.fori_loop(0, ANGLES // TILE, choose, 0)

    rows_at_once = 32

    def tables(step, carry):
        first = pl.multiple_of(step * rows_at_once, rows_at_once)
        angle = lax.broadcasted_iota(jnp.int32, (rows_at_once, BINS), 0) + first
        angle_pos = (angle.astype(jnp.float32) + 0.5) / ANGLES - 0.5
        bins = lax.broadcasted_iota(jnp.int32, (rows_at_once, BINS), 1) + block * BINS
        range_pos = 1.0 + bins.astype(jnp.float32) / total_bins
        for level in range(LEVELS):
            for side, owner in enumerate((group, partners[level])):
                phase = math.pi * shifts[level, owner] * angle_pos * range_pos
                cos_table[level, side, pl.ds(first, rows_at_once), :] = jnp.cos(phase)
                sin_table[level, side, pl.ds(first, rows_at_once), :] = jnp.sin(phase)
        return carry

    lax.fori_loop(0, ANGLES // rows_at_once, tables, 0)

    @pl.when(block == 0)
    def _():
        for level in range(LEVELS):
            left_rim[level] = jnp.zeros((2 * ANGLES, TILE), jnp.bfloat16)

    @pl.when(block == sources - 1)
    def _():
        for level in range(LEVELS):
            right_rim[level] = jnp.zeros((2 * ANGLES, TILE), jnp.bfloat16)

    def to_left(level):
        return pltpu.make_async_remote_copy(
            src_ref=images.at[level, :, pl.ds(0, TILE)],
            dst_ref=right_rim.at[level],
            send_sem=rim_send.at[level, 0],
            recv_sem=rim_recv.at[level, 0],
            device_id=(group, block - 1),
            device_id_type=MESH,
        )

    def to_right(level):
        return pltpu.make_async_remote_copy(
            src_ref=images.at[level, :, pl.ds(BINS - TILE, TILE)],
            dst_ref=left_rim.at[level],
            send_sem=rim_send.at[level, 1],
            recv_sem=rim_recv.at[level, 1],
            device_id=(group, block + 1),
            device_id_type=MESH,
        )

    def send_rims(level, left=True, right=True):
        if left:

            @pl.when(block > 0)
            def _():
                to_left(level).start()

        if right:

            @pl.when(block < sources - 1)
            def _():
                to_right(level).start()

    load.wait()
    stay.wait()
    others = turned.at[pl.ds(0, sources - 1)]
    pltpu.make_async_copy(others, others, turn_sem.at[1]).wait()
    pltpu.make_async_copy(others, others, turn_sem.at[0]).wait()

    def filtering(step, carry):
        start = pl.multiple_of(step * TILE, TILE)
        stack = turned[...].reshape(2 * PULSES, BINS)
        image = jnp.dot(wide[pl.ds(start, TILE), :], stack, preferred_element_type=jnp.float32)
        images[0, pl.ds(start, TILE), :] = image.astype(jnp.bfloat16)
        return carry

    lax.fori_loop(0, 2 * ANGLES // TILE, filtering, 0)
    send_rims(0)

    for level in range(LEVELS):
        flag = flags[level, group]

        def split(values):
            side = jnp.full(values[0].shape, flag, jnp.int32)
            give = jnp.where(side == 1, values[0], values[1]).astype(jnp.bfloat16)
            keep = jnp.where(side == 1, values[1], values[0]).astype(jnp.bfloat16)
            return give, keep

        def rows_of(part):
            return [slice(part * ANGLES + side * HALF, part * ANGLES + side * HALF + HALF) for side in range(2)]

        def middle(part, level=level):
            return [
                jnp.dot(
                    images[level, rows, :],
                    shifted[level, TILE : TILE + BINS, TILE : 3 * TILE],
                    preferred_element_type=jnp.float32,
                )
                for rows in rows_of(part)
            ]

        def first(part, level=level):
            return [
                jnp.dot(
                    images[level, rows, 0 : 2 * TILE],
                    shifted[level, TILE : 3 * TILE, 0:TILE],
                    preferred_element_type=jnp.float32,
                )
                + jnp.dot(left_rim[level, rows, :], shifted[level, 0:TILE, 0:TILE], preferred_element_type=jnp.float32)
                for rows in rows_of(part)
            ]

        def last(part, level=level):
            return [
                jnp.dot(
                    images[level, rows, BINS - 2 * TILE : BINS],
                    shifted[level, BINS - TILE : BINS + TILE, BINS - TILE : BINS],
                    preferred_element_type=jnp.float32,
                )
                + jnp.dot(
                    right_rim[level, rows, :],
                    shifted[level, BINS + TILE : BINS + 2 * TILE, BINS - TILE : BINS],
                    preferred_element_type=jnp.float32,
                )
                for rows in rows_of(part)
            ]

        def to_partner(tile, level=level):
            return pltpu.make_async_remote_copy(
                src_ref=given.at[level, tile],
                dst_ref=taken.at[level, tile],
                send_sem=pair_send.at[level, tile],
                recv_sem=pair_recv.at[level, tile],
                device_id=(partners[level], block),
                device_id_type=MESH,
            )

        for part in range(2):
            give, keep = split(middle(part))
            given[level, 1, part] = give[:, 0:TILE]
            given[level, 2, part] = give[:, TILE : 2 * TILE]
            kept[part, :, TILE : 3 * TILE] = keep
        to_partner(1).start()
        to_partner(2).start()

        @pl.when(block > 0)
        def _(level=level):
            to_right(level).wait_recv()

        for part in range(2):
            given[level, 0, part], kept[part, :, 0:TILE] = split(first(part))
        to_partner(0).start()

        @pl.when(block < sources - 1)
        def _(level=level):
            to_left(level).wait_recv()

        for part in range(2):
            given[level, 3, part], kept[part, :, BINS - TILE : BINS] = split(last(part))
        to_partner(3).start()

        def own(step, carry, level=level):
            rows = pl.ds(pl.multiple_of(step * TILE, TILE), TILE)
            low_rows = pl.ds(pl.multiple_of(step * TILE + ANGLES, TILE), TILE)
            matrix = chosen[level, 0, rows, :]
            real = jnp.dot(matrix, kept[0], preferred_element_type=jnp.float32)
            imag = jnp.dot(matrix, kept[1], preferred_element_type=jnp.float32)
            cosine = cos_table[level, 0, rows, :]
            sine = sin_table[level, 0, rows, :]
            total[rows, :] = real * cosine - imag * sine
            total[low_rows, :] = real * sine + imag * cosine
            return carry

        lax.fori_loop(0, ANGLES // TILE, own, 0)

        for tile in ORDER:
            columns = slice(tile * TILE, tile * TILE + TILE)
            to_partner(tile).wait_recv()

            def theirs(step, carry, level=level, tile=tile, columns=columns):
                rows = pl.ds(pl.multiple_of(step * TILE, TILE), TILE)
                low_rows = pl.ds(pl.multiple_of(step * TILE + ANGLES, TILE), TILE)
                matrix = chosen[level, 1, rows, :]
                real = jnp.dot(matrix, taken[level, tile, 0], preferred_element_type=jnp.float32)
                imag = jnp.dot(matrix, taken[level, tile, 1], preferred_element_type=jnp.float32)
                cosine = cos_table[level, 1, rows, columns]
                sine = sin_table[level, 1, rows, columns]
                high = total[rows, columns] + (real * cosine - imag * sine)
                low = total[low_rows, columns] + (real * sine + imag * cosine)
                if level + 1 < LEVELS:
                    images[level + 1, rows, columns] = high.astype(jnp.bfloat16)
                    images[level + 1, low_rows, columns] = low.astype(jnp.bfloat16)
                else:
                    total[rows, columns] = high
                    total[low_rows, columns] = low
                return carry

            lax.fori_loop(0, ANGLES // TILE, theirs, 0)
            if level + 1 < LEVELS:
                send_rims(level + 1, left=tile == 0, right=tile == TILES - 1)
            else:
                for part in range(2):
                    pltpu.make_async_copy(
                        total.at[pl.ds(part * ANGLES, ANGLES), pl.ds(tile * TILE, TILE)],
                        out.at[part, :, pl.ds(tile * TILE, TILE)],
                        out_sem.at[part, tile],
                    ).start()

        for tile in ORDER:
            to_partner(tile).wait_send()

        @pl.when(block > 0)
        def _(level=level):
            to_left(level).wait_send()

        @pl.when(block < sources - 1)
        def _(level=level):
            to_right(level).wait_send()

    for tile in range(TILES):
        for part in range(2):
            pltpu.make_async_copy(
                total.at[pl.ds(part * ANGLES, ANGLES), pl.ds(tile * TILE, TILE)],
                out.at[part, :, pl.ds(tile * TILE, TILE)],
                out_sem.at[part, tile],
            ).wait()


def on_device(doppler, sources, echoes, fore_flag, band_offset, angle_interp, range_kernel, center_shift):
    pulses = echoes.shape[1]
    total_bins = echoes.shape[2]
    any_space = pl.BlockSpec(memory_space=pl.ANY)
    vmem = pl.BlockSpec(memory_space=pltpu.VMEM)
    smem = pl.BlockSpec(memory_space=pltpu.SMEM)
    bf16 = jnp.bfloat16
    return pl.pallas_call(
        functools.partial(kernel, sources, total_bins),
        out_shape=jax.ShapeDtypeStruct((2, ANGLES, BINS), jnp.float32),
        in_specs=[any_space, any_space, vmem, vmem, smem, smem, smem],
        out_specs=any_space,
        scratch_shapes=[
            pltpu.VMEM((sources, 2 * pulses, BINS), bf16),
            pltpu.VMEM((2 * ANGLES, 2 * PULSES), bf16),
            pltpu.VMEM((LEVELS, BINS + 2 * TILE, BINS), bf16),
            pltpu.VMEM((LEVELS, 2, ANGLES, HALF), bf16),
            pltpu.VMEM((LEVELS, 2 * ANGLES, BINS), bf16),
            pltpu.VMEM((LEVELS, 2 * ANGLES, TILE), bf16),
            pltpu.VMEM((LEVELS, 2 * ANGLES, TILE), bf16),
            pltpu.VMEM((LEVELS, TILES, 2, HALF, TILE), bf16),
            pltpu.VMEM((2, HALF, BINS), bf16),
            pltpu.VMEM((LEVELS, TILES, 2, HALF, TILE), bf16),
            pltpu.VMEM((2 * ANGLES, BINS), jnp.float32),
            pltpu.VMEM((LEVELS, 2, ANGLES, BINS), jnp.float32),
            pltpu.VMEM((LEVELS, 2, ANGLES, BINS), jnp.float32),
            pltpu.SemaphoreType.DMA((3,)),
            pltpu.SemaphoreType.DMA,
            pltpu.SemaphoreType.DMA((LEVELS, 2)),
            pltpu.SemaphoreType.DMA((LEVELS, 2)),
            pltpu.SemaphoreType.DMA((LEVELS, TILES)),
            pltpu.SemaphoreType.DMA((LEVELS, TILES)),
            pltpu.SemaphoreType.DMA((2, TILES)),
        ],
        compiler_params=pltpu.CompilerParams(collective_id=0, has_side_effects=True, vmem_limit_bytes=60 * 2**20),
    )(
        echoes.reshape(2 * pulses, total_bins),
        jnp.asarray(doppler),
        range_kernel,
        angle_interp,
        fore_flag[:, :, 0],
        band_offset[:, :, 0],
        center_shift,
    )


def solution(mesh):
    sources = mesh.shape["rng"]
    placed = (
        P(None, ("sub", "rng"), None),
        P(None, None, "rng"),
        P(None, None, "rng"),
        P(),
        P(),
        P(),
    )
    body = functools.partial(on_device, doppler_constant(sources), sources)
    return jax.shard_map(body, mesh=mesh, in_specs=placed, out_specs=P(None, "sub", "rng"), check_vma=False)
```

time: 295 us -> 150 us (0.51)
  the two profiles are of different devices: /device:TPU:31 before, /device:TPU:39 now
where the time goes in v1:
time: 150 us
  Pallas kernels  145 us (97%)
  local copies, waits for them, and re-layouts  4.36 us (3%)
    pallas_call x1, Pallas kernels, on_device(): pl.pallas_call(functools.partial(kernel, sources, total_bins), out_shape=...  145 us
    unnamed x2, local copies, waits for them, and re-layouts  4.36 us

profile of v1, /device:TPU:39, one launch (start us, length us, event | category | flops | bytes accessed | tf_op | source)
XLA Modules:
  0.0 149.5 jit_solution(11819157088804143733)
XLA Ops:
  0.0 1.3 copy_bitcast_fusion
  1.3 145.1 %shard_map.73 = f32[2,512,512]{2,1,0:T(8,128)} custom-call(bf16[16,32768]{1,0:T(8,128)(2,1)} %bitcast.5, bf16[1024,1024]{1,0:T(8,128)(2,1)} %constant.2.clone.doppler, bf16[3,544,512]{2,1,0:T(8,128)(2,1)} %kernels.1, bf16[3,2,512,256]{3,2,1,0:T(8,128)(2,1)} %interp.1, s32[3,8]{1,0:T(4,128)} %get-tuple-element.6.flags, s32[3,8]{1,0:T(4,128)} %get-tuple-element.5.offsets, ...), custom_call_target="tpu_custom_call" | custom-call | tf_op jit(solution)/shard_map/pallas_call | solution.py:362
  146.4 3.1 %copy.13 = f32[2,512,512]{2,1,0:T(8,128)} copy(f32[2,512,512]{2,1,0:T(8,128)} %shard_map.73) | data formatting | bytes 4194304

commit v2 on v1

--- a/solution.py
+++ b/solution.py
@@ -19,7 +19,7 @@
 BAND_HALF = 16
 LEVELS = 3
 MESH = pl.DeviceIdType.MESH
-ORDER = (1, 2, 0, 3)
+ORDERS = ((1, 2, 3, 0), (2, 1, 0, 3), (1, 2, 3, 0))
 
 
 def doppler_constant(sources):
@@ -39,14 +39,16 @@
     total_bins,
     echoes,
     doppler,
-    kernels,
-    interp,
+    kernels_far,
+    interp_far,
     flags,
     offsets,
     shifts,
     out,
     turned,
     wide,
+    kernels,
+    interp,
     shifted,
     chosen,
     images,
@@ -80,8 +82,12 @@
     for partner in partners[::-1]:
         pl.semaphore_signal(barrier, inc=1, device_id=(partner, block), device_id_type=MESH)
     lax.fori_loop(1, sources, greet, 0)
-    load = pltpu.make_async_copy(doppler, wide, wide_sem)
-    load.start()
+    loads = [
+        pltpu.make_async_copy(source, target, wide_sem.at[place])
+        for place, (source, target) in enumerate(((kernels_far, kernels), (interp_far, interp), (doppler, wide)))
+    ]
+    for load in loads:
+        load.start()
     pl.semaphore_wait(barrier, sources - 1 + LEVELS)
 
     def turn(step, carry):
@@ -102,8 +108,10 @@
     )
     stay.start()
 
+    loads[0].wait()
+    loads[1].wait()
     for level in range(LEVELS):
-        offset = offsets[level, group]
+        offset = offsets[level, 0, group]
         rows = lax.broadcasted_iota(jnp.int32, (TILE, BINS + 2 * BAND_HALF), 0)
         taps = lax.broadcasted_iota(jnp.int32, (TILE, BINS + 2 * BAND_HALF), 1)
 
@@ -120,7 +128,7 @@
             rows = pl.ds(pl.multiple_of(step * TILE, TILE), TILE)
             zero = interp[level, 0, rows, :].astype(jnp.float32)
             one = interp[level, 1, rows, :].astype(jnp.float32)
-            side = jnp.full((TILE, HALF), flags[level, group], jnp.int32)
+            side = jnp.full((TILE, HALF), flags[level, 0, group], jnp.int32)
             chosen[level, 0, rows, :] = jnp.where(side == 1, one, zero).astype(jnp.bfloat16)
             chosen[level, 1, rows, :] = jnp.where(side == 1, zero, one).astype(jnp.bfloat16)
             return carry
@@ -187,11 +195,10 @@
             def _():
                 to_right(level).start()
 
-    load.wait()
+    loads[2].wait()
     stay.wait()
     others = turned.at[pl.ds(0, sources - 1)]
     pltpu.make_async_copy(others, others, turn_sem.at[1]).wait()
-    pltpu.make_async_copy(others, others, turn_sem.at[0]).wait()
 
     def filtering(step, carry):
         start = pl.multiple_of(step * TILE, TILE)
@@ -203,88 +210,57 @@
     lax.fori_loop(0, 2 * ANGLES // TILE, filtering, 0)
     send_rims(0)
 
+    def to_partner(level, tile):
+        return pltpu.make_async_remote_copy(
+            src_ref=given.at[level, tile],
+            dst_ref=taken.at[level, tile],
+            send_sem=pair_send.at[level, tile],
+            recv_sem=pair_recv.at[level, tile],
+            device_id=(partners[level], block),
+            device_id_type=MESH,
+        )
+
+    def resample(level, tile):
+        if tile == 0:
+
+            @pl.when(block > 0)
+            def _():
+                to_right(level).wait_recv()
+
+        if tile == TILES - 1:
+
+            @pl.when(block < sources - 1)
+            def _():
+                to_left(level).wait_recv()
+
+        columns = slice(tile * TILE, tile * TILE + TILE)
+        weights = shifted[level, tile * TILE : (tile + 3) * TILE, columns]
+        flag = jnp.full((HALF, TILE), flags[level, 0, group], jnp.int32)
+        for part in range(2):
+            values = []
+            for side in range(2):
+                rows = slice(part * ANGLES + side * HALF, part * ANGLES + side * HALF + HALF)
+                if tile == 0:
+                    window = jnp.concatenate([left_rim[level, rows, :], images[level, rows, 0 : 2 * TILE]], axis=1)
+                elif tile == TILES - 1:
+                    window = jnp.concatenate([images[level, rows, BINS - 2 * TILE :], right_rim[level, rows, :]], axis=1)
+                else:
+                    window = images[level, rows, (tile - 1) * TILE : (tile + 2) * TILE]
+                values.append(jnp.dot(window, weights, preferred_element_type=jnp.float32))
+            given[level, tile, part] = jnp.where(flag == 1, values[0], values[1]).astype(jnp.bfloat16)
+            kept[part, :, columns] = jnp.where(flag == 1, values[1], values[0]).astype(jnp.bfloat16)
+        to_partner(level, tile).start()
+
+    def to_out(part, tile):
+        return pltpu.make_async_copy(
+            total.at[pl.ds(part * ANGLES, ANGLES), pl.ds(tile * TILE, TILE)],
+            out.at[part, :, pl.ds(tile * TILE, TILE)],
+            out_sem.at[part, tile],
+        )
+
+    for tile in ORDERS[0]:
+        resample(0, tile)
     for level in range(LEVELS):
-        flag = flags[level, group]
-
-        def split(values):
-            side = jnp.full(values[0].shape, flag, jnp.int32)
-            give = jnp.where(side == 1, values[0], values[1]).astype(jnp.bfloat16)
-            keep = jnp.where(side == 1, values[1], values[0]).astype(jnp.bfloat16)
-            return give, keep
-
-        def rows_of(part):
-            return [slice(part * ANGLES + side * HALF, part * ANGLES + side * HALF + HALF) for side in range(2)]
-
-        def middle(part, level=level):
-            return [
-                jnp.dot(
-                    images[level, rows, :],
-                    shifted[level, TILE : TILE + BINS, TILE : 3 * TILE],
-                    preferred_element_type=jnp.float32,
-                )
-                for rows in rows_of(part)
-            ]
-
-        def first(part, level=level):
-            return [
-                jnp.dot(
-                    images[level, rows, 0 : 2 * TILE],
-                    shifted[level, TILE : 3 * TILE, 0:TILE],
-                    preferred_element_type=jnp.float32,
-                )
-                + jnp.dot(left_rim[level, rows, :], shifted[level, 0:TILE, 0:TILE], preferred_element_type=jnp.float32)
-                for rows in rows_of(part)
-            ]
-
-        def last(part, level=level):
-            return [
-                jnp.dot(
-                    images[level, rows, BINS - 2 * TILE : BINS],
-                    shifted[level, BINS - TILE : BINS + TILE, BINS - TILE : BINS],
-                    preferred_element_type=jnp.float32,
-                )
-                + jnp.dot(
-                    right_rim[level, rows, :],
-                    shifted[level, BINS + TILE : BINS + 2 * TILE, BINS - TILE : BINS],
-                    preferred_element_type=jnp.float32,
-                )
-                for rows in rows_of(part)
-            ]
-
-        def to_partner(tile, level=level):
-            return pltpu.make_async_remote_copy(
-                src_ref=given.at[level, tile],
-                dst_ref=taken.at[level, tile],
-                send_sem=pair_send.at[level, tile],
-                recv_sem=pair_recv.at[level, tile],
-                device_id=(partners[level], block),
-                device_id_type=MESH,
-            )
-
-        for part in range(2):
-            give, keep = split(middle(part))
-            given[level, 1, part] = give[:, 0:TILE]
-            given[level, 2, part] = give[:, TILE : 2 * TILE]
-            kept[part, :, TILE : 3 * TILE] = keep
-        to_partner(1).start()
-        to_partner(2).start()
-
-        @pl.when(block > 0)
-        def _(level=level):
-            to_right(level).wait_recv()
-
-        for part in range(2):
-            given[level, 0, part], kept[part, :, 0:TILE] = split(first(part))
-        to_partner(0).start()
-
-        @pl.when(block < sources - 1)
-        def _(level=level):
-            to_left(level).wait_recv()
-
-        for part in range(2):
-            given[level, 3, part], kept[part, :, BINS - TILE : BINS] = split(last(part))
-        to_partner(3).start()
-
         def own(step, carry, level=level):
             rows = pl.ds(pl.multiple_of(step * TILE, TILE), TILE)
             low_rows = pl.ds(pl.multiple_of(step * TILE + ANGLES, TILE), TILE)
@@ -299,9 +275,9 @@
 
         lax.fori_loop(0, ANGLES // TILE, own, 0)
 
-        for tile in ORDER:
+        for order, tile in enumerate(ORDERS[level]):
             columns = slice(tile * TILE, tile * TILE + TILE)
-            to_partner(tile).wait_recv()
+            to_partner(level, tile).wait_recv()
 
             def theirs(step, carry, level=level, tile=tile, columns=columns):
                 rows = pl.ds(pl.multiple_of(step * TILE, TILE), TILE)
@@ -324,16 +300,18 @@
             lax.fori_loop(0, ANGLES // TILE, theirs, 0)
             if level + 1 < LEVELS:
                 send_rims(level + 1, left=tile == 0, right=tile == TILES - 1)
+                if order == 2:
+                    resample(level + 1, ORDERS[level + 1][0])
+                if order == 3:
+                    for later in ORDERS[level + 1][1:]:
+                        resample(level + 1, later)
             else:
                 for part in range(2):
-                    pltpu.make_async_copy(
-                        total.at[pl.ds(part * ANGLES, ANGLES), pl.ds(tile * TILE, TILE)],
-                        out.at[part, :, pl.ds(tile * TILE, TILE)],
-                        out_sem.at[part, tile],
-                    ).start()
-
-        for tile in ORDER:
-            to_partner(tile).wait_send()
+                    to_out(part, tile).start()
+
+    for level in range(LEVELS):
+        for tile in range(TILES):
+            to_partner(level, tile).wait_send()
 
         @pl.when(block > 0)
         def _(level=level):
@@ -343,30 +321,28 @@
         def _(level=level):
             to_right(level).wait_send()
 
+    pltpu.make_async_copy(others, others, turn_sem.at[0]).wait()
     for tile in range(TILES):
         for part in range(2):
-            pltpu.make_async_copy(
-                total.at[pl.ds(part * ANGLES, ANGLES), pl.ds(tile * TILE, TILE)],
-                out.at[part, :, pl.ds(tile * TILE, TILE)],
-                out_sem.at[part, tile],
-            ).wait()
+            to_out(part, tile).wait()
 
 
 def on_device(doppler, sources, echoes, fore_flag, band_offset, angle_interp, range_kernel, center_shift):
     pulses = echoes.shape[1]
     total_bins = echoes.shape[2]
     any_space = pl.BlockSpec(memory_space=pl.ANY)
-    vmem = pl.BlockSpec(memory_space=pltpu.VMEM)
     smem = pl.BlockSpec(memory_space=pltpu.SMEM)
     bf16 = jnp.bfloat16
     return pl.pallas_call(
         functools.partial(kernel, sources, total_bins),
         out_shape=jax.ShapeDtypeStruct((2, ANGLES, BINS), jnp.float32),
-        in_specs=[any_space, any_space, vmem, vmem, smem, smem, smem],
+        in_specs=[any_space, any_space, any_space, any_space, smem, smem, smem],
         out_specs=any_space,
         scratch_shapes=[
             pltpu.VMEM((sources, 2 * pulses, BINS), bf16),
             pltpu.VMEM((2 * ANGLES, 2 * PULSES), bf16),
+            pltpu.VMEM(range_kernel.shape, bf16),
+            pltpu.VMEM(angle_interp.shape, bf16),
             pltpu.VMEM((LEVELS, BINS + 2 * TILE, BINS), bf16),
             pltpu.VMEM((LEVELS, 2, ANGLES, HALF), bf16),
             pltpu.VMEM((LEVELS, 2 * ANGLES, BINS), bf16),
@@ -379,7 +355,7 @@
             pltpu.VMEM((LEVELS, 2, ANGLES, BINS), jnp.float32),
             pltpu.VMEM((LEVELS, 2, ANGLES, BINS), jnp.float32),
             pltpu.SemaphoreType.DMA((3,)),
-            pltpu.SemaphoreType.DMA,
+            pltpu.SemaphoreType.DMA((3,)),
             pltpu.SemaphoreType.DMA((LEVELS, 2)),
             pltpu.SemaphoreType.DMA((LEVELS, 2)),
             pltpu.SemaphoreType.DMA((LEVELS, TILES)),
@@ -392,8 +368,8 @@
         jnp.asarray(doppler),
         range_kernel,
         angle_interp,
-        fore_flag[:, :, 0],
-        band_offset[:, :, 0],
+        fore_flag.transpose(0, 2, 1),
+        band_offset.transpose(0, 2, 1),
         center_shift,
     )
 

time: 150 us -> 148 us (0.987)
  the two profiles are of different devices: /device:TPU:39 before, /device:TPU:128 now
where the time goes in v2:
time: 148 us
  Pallas kernels  145 us (98%)
  local copies, waits for them, and re-layouts  3.08 us (2%)
    pallas_call x1, Pallas kernels, on_device(): pl.pallas_call(functools.partial(kernel, sources, total_bins), out_shape=...  145 us
    unnamed x1, local copies, waits for them, and re-layouts  3.08 us

profile of v2, /device:TPU:128, one launch (start us, length us, event | category | flops | bytes accessed | tf_op | source)
XLA Modules:
  0.0 147.6 jit_solution(5148223871948184161)
XLA Ops:
  0.0 144.5 %shard_map.73 = f32[2,512,512]{2,1,0:T(8,128)} custom-call(bf16[16,32768]{1,0:T(8,128)(2,1)} %bitcast.3, bf16[1024,1024]{1,0:T(8,128)(2,1)} %constant.2.clone.doppler, bf16[3,544,512]{2,1,0:T(8,128)(2,1)} %kernels_far.1, bf16[3,2,512,256]{3,2,1,0:T(8,128)(2,1)} %interp_far.1, s32[3,1,8]{2,1,0:T(1,128)} %bitcast.4, s32[3,1,8]{2,1,0:T(1,128)} %bitcast.5, ...), custom_call_target="tpu_custom_call" | custom-call | tf_op jit(solution)/shard_map/pallas_call | solution.py:336
  144.5 3.1 %copy.9 = f32[2,512,512]{2,1,0:T(8,128)} copy(f32[2,512,512]{2,1,0:T(8,128)} %shard_map.73) | data formatting | bytes 4194304

commit v3 on v2

--- a/solution.py
+++ b/solution.py
@@ -46,6 +46,7 @@
     shifts,
     out,
     turned,
+    turned_last,
     wide,
     kernels,
     interp,
@@ -90,23 +91,35 @@
         load.start()
     pl.semaphore_wait(barrier, sources - 1 + LEVELS)
 
-    def turn(step, carry):
-        peer = lax.rem(block + step, sources)
-        pltpu.make_async_remote_copy(
-            src_ref=echoes.at[:, pl.ds(pl.multiple_of(peer * BINS, BINS), BINS)],
-            dst_ref=turned.at[block],
-            send_sem=turn_sem.at[0],
-            recv_sem=turn_sem.at[1],
-            device_id=(group, peer),
-            device_id_type=MESH,
-        ).start()
-        return carry
-
-    lax.fori_loop(1, sources, turn, 0)
-    stay = pltpu.make_async_copy(
-        echoes.at[:, pl.ds(pl.multiple_of(block * BINS, BINS), BINS)], turned.at[block], turn_sem.at[2]
-    )
-    stay.start()
+    rounds = ((turned, 0, BINS - TILE), (turned_last, BINS - TILE, TILE))
+
+    def columns_of(owner, start, width):
+        return pl.ds(pl.multiple_of(owner * BINS + start, TILE), width)
+
+    for place, (target, start, width) in enumerate(rounds):
+
+        def turn(step, carry, place=place, target=target, start=start, width=width):
+            peer = lax.rem(block + step, sources)
+            pltpu.make_async_remote_copy(
+                src_ref=echoes.at[:, columns_of(peer, start, width)],
+                dst_ref=target.at[block],
+                send_sem=turn_sem.at[place, 0],
+                recv_sem=turn_sem.at[place, 1],
+                device_id=(group, peer),
+                device_id_type=MESH,
+            ).start()
+            return carry
+
+        lax.fori_loop(1, sources, turn, 0)
+
+    def stay(place):
+        target, start, width = rounds[place]
+        return pltpu.make_async_copy(
+            echoes.at[:, columns_of(block, start, width)], target.at[block], turn_sem.at[place, 2]
+        )
+
+    stay(0).start()
+    stay(1).start()
 
     loads[0].wait()
     loads[1].wait()
@@ -137,20 +150,23 @@
 
     rows_at_once = 32
 
-    def tables(step, carry):
+    def tables(step, carry, levels):
         first = pl.multiple_of(step * rows_at_once, rows_at_once)
         angle = lax.broadcasted_iota(jnp.int32, (rows_at_once, BINS), 0) + first
         angle_pos = (angle.astype(jnp.float32) + 0.5) / ANGLES - 0.5
         bins = lax.broadcasted_iota(jnp.int32, (rows_at_once, BINS), 1) + block * BINS
         range_pos = 1.0 + bins.astype(jnp.float32) / total_bins
-        for level in range(LEVELS):
+        for level in levels:
             for side, owner in enumerate((group, partners[level])):
                 phase = math.pi * shifts[level, owner] * angle_pos * range_pos
                 cos_table[level, side, pl.ds(first, rows_at_once), :] = jnp.cos(phase)
                 sin_table[level, side, pl.ds(first, rows_at_once), :] = jnp.sin(phase)
         return carry
 
-    lax.fori_loop(0, ANGLES // rows_at_once, tables, 0)
+    def make_tables(*levels):
+        lax.fori_loop(0, ANGLES // rows_at_once, functools.partial(tables, levels=levels), 0)
+
+    make_tables(0, 1)
 
     @pl.when(block == 0)
     def _():
@@ -196,19 +212,24 @@
                 to_right(level).start()
 
     loads[2].wait()
-    stay.wait()
-    others = turned.at[pl.ds(0, sources - 1)]
-    pltpu.make_async_copy(others, others, turn_sem.at[1]).wait()
-
-    def filtering(step, carry):
-        start = pl.multiple_of(step * TILE, TILE)
-        stack = turned[...].reshape(2 * PULSES, BINS)
-        image = jnp.dot(wide[pl.ds(start, TILE), :], stack, preferred_element_type=jnp.float32)
-        images[0, pl.ds(start, TILE), :] = image.astype(jnp.bfloat16)
-        return carry
-
-    lax.fori_loop(0, 2 * ANGLES // TILE, filtering, 0)
-    send_rims(0)
+
+    def others(place):
+        target = rounds[place][0].at[pl.ds(0, sources - 1)]
+        return [pltpu.make_async_copy(target, target, turn_sem.at[place, side]) for side in range(2)]
+
+    def filter_round(place):
+        target, first, width = rounds[place]
+        stay(place).wait()
+        others(place)[1].wait()
+
+        def filtering(step, carry):
+            start = pl.multiple_of(step * TILE, TILE)
+            stack = target[...].reshape(2 * PULSES, width)
+            image = jnp.dot(wide[pl.ds(start, TILE), :], stack, preferred_element_type=jnp.float32)
+            images[0, pl.ds(start, TILE), first : first + width] = image.astype(jnp.bfloat16)
+            return carry
+
+        lax.fori_loop(0, 2 * ANGLES // TILE, filtering, 0)
 
     def to_partner(level, tile):
         return pltpu.make_async_remote_copy(
@@ -258,9 +279,17 @@
             out_sem.at[part, tile],
         )
 
-    for tile in ORDERS[0]:
+    filter_round(0)
+    send_rims(0, right=False)
+    resample(0, ORDERS[0][0])
+    filter_round(1)
+    send_rims(0, left=False)
+    for tile in ORDERS[0][1:]:
         resample(0, tile)
     for level in range(LEVELS):
+        if level == LEVELS - 1:
+            make_tables(level)
+
         def own(step, carry, level=level):
             rows = pl.ds(pl.multiple_of(step * TILE, TILE), TILE)
             low_rows = pl.ds(pl.multiple_of(step * TILE + ANGLES, TILE), TILE)
@@ -321,7 +350,8 @@
         def _(level=level):
             to_right(level).wait_send()
 
-    pltpu.make_async_copy(others, others, turn_sem.at[0]).wait()
+    for place in range(2):
+        others(place)[0].wait()
     for tile in range(TILES):
         for part in range(2):
             to_out(part, tile).wait()
@@ -339,7 +369,8 @@
         in_specs=[any_space, any_space, any_space, any_space, smem, smem, smem],
         out_specs=any_space,
         scratch_shapes=[
-            pltpu.VMEM((sources, 2 * pulses, BINS), bf16),
+            pltpu.VMEM((sources, 2 * pulses, BINS - TILE), bf16),
+            pltpu.VMEM((sources, 2 * pulses, TILE), bf16),
             pltpu.VMEM((2 * ANGLES, 2 * PULSES), bf16),
             pltpu.VMEM(range_kernel.shape, bf16),
             pltpu.VMEM(angle_interp.shape, bf16),
@@ -354,7 +385,7 @@
             pltpu.VMEM((2 * ANGLES, BINS), jnp.float32),
             pltpu.VMEM((LEVELS, 2, ANGLES, BINS), jnp.float32),
             pltpu.VMEM((LEVELS, 2, ANGLES, BINS), jnp.float32),
-            pltpu.SemaphoreType.DMA((3,)),
+            pltpu.SemaphoreType.DMA((2, 3)),
             pltpu.SemaphoreType.DMA((3,)),
             pltpu.SemaphoreType.DMA((LEVELS, 2)),
             pltpu.SemaphoreType.DMA((LEVELS, 2)),

time: 148 us -> 149 us (level)
  the two profiles are of different devices: /device:TPU:128 before, /device:TPU:175 now
where the time goes in v3:
time: 149 us
  Pallas kernels  146 us (98%)
  local copies, waits for them, and re-layouts  3.08 us (2%)
    pallas_call x1, Pallas kernels, on_device(): pl.pallas_call(functools.partial(kernel, sources, total_bins), out_shape=...  146 us
    unnamed x1, local copies, waits for them, and re-layouts  3.08 us

profile of v3, /device:TPU:175, one launch (start us, length us, event | category | flops | bytes accessed | tf_op | source)
XLA Modules:
  0.0 149.3 jit_solution(4540570428363271563)
XLA Ops:
  0.0 146.2 %shard_map.73 = f32[2,512,512]{2,1,0:T(8,128)} custom-call(bf16[16,32768]{1,0:T(8,128)(2,1)} %bitcast.3, bf16[1024,1024]{1,0:T(8,128)(2,1)} %constant.2.clone.doppler, bf16[3,544,512]{2,1,0:T(8,128)(2,1)} %kernels_far.1, bf16[3,2,512,256]{3,2,1,0:T(8,128)(2,1)} %interp_far.1, s32[3,1,8]{2,1,0:T(1,128)} %bitcast.4, s32[3,1,8]{2,1,0:T(1,128)} %bitcast.5, ...), custom_call_target="tpu_custom_call" | custom-call | tf_op jit(solution)/shard_map/pallas_call | solution.py:366
  146.2 3.1 %copy.9 = f32[2,512,512]{2,1,0:T(8,128)} copy(f32[2,512,512]{2,1,0:T(8,128)} %shard_map.73) | data formatting | bytes 4194304

commit v4 on v2

--- a/solution.py
+++ b/solution.py
@@ -200,14 +200,10 @@
     others = turned.at[pl.ds(0, sources - 1)]
     pltpu.make_async_copy(others, others, turn_sem.at[1]).wait()
 
-    def filtering(step, carry):
-        start = pl.multiple_of(step * TILE, TILE)
-        stack = turned[...].reshape(2 * PULSES, BINS)
-        image = jnp.dot(wide[pl.ds(start, TILE), :], stack, preferred_element_type=jnp.float32)
-        images[0, pl.ds(start, TILE), :] = image.astype(jnp.bfloat16)
-        return carry
-
-    lax.fori_loop(0, 2 * ANGLES // TILE, filtering, 0)
+    for part in range(2):
+        rows = slice(part * ANGLES, part * ANGLES + ANGLES)
+        image = jnp.dot(wide[rows, :], turned[...].reshape(2 * PULSES, BINS), preferred_element_type=jnp.float32)
+        images[0, rows, :] = image.astype(jnp.bfloat16)
     send_rims(0)
 
     def to_partner(level, tile):
@@ -237,16 +233,15 @@
         weights = shifted[level, tile * TILE : (tile + 3) * TILE, columns]
         flag = jnp.full((HALF, TILE), flags[level, 0, group], jnp.int32)
         for part in range(2):
-            values = []
-            for side in range(2):
-                rows = slice(part * ANGLES + side * HALF, part * ANGLES + side * HALF + HALF)
-                if tile == 0:
-                    window = jnp.concatenate([left_rim[level, rows, :], images[level, rows, 0 : 2 * TILE]], axis=1)
-                elif tile == TILES - 1:
-                    window = jnp.concatenate([images[level, rows, BINS - 2 * TILE :], right_rim[level, rows, :]], axis=1)
-                else:
-                    window = images[level, rows, (tile - 1) * TILE : (tile + 2) * TILE]
-                values.append(jnp.dot(window, weights, preferred_element_type=jnp.float32))
+            rows = slice(part * ANGLES, part * ANGLES + ANGLES)
+            if tile == 0:
+                window = jnp.concatenate([left_rim[level, rows, :], images[level, rows, 0 : 2 * TILE]], axis=1)
+            elif tile == TILES - 1:
+                window = jnp.concatenate([images[level, rows, BINS - 2 * TILE :], right_rim[level, rows, :]], axis=1)
+            else:
+                window = images[level, rows, (tile - 1) * TILE : (tile + 2) * TILE]
+            both = jnp.dot(window, weights, preferred_element_type=jnp.float32)
+            values = (both[0:HALF], both[HALF:ANGLES])
             given[level, tile, part] = jnp.where(flag == 1, values[0], values[1]).astype(jnp.bfloat16)
             kept[part, :, columns] = jnp.where(flag == 1, values[1], values[0]).astype(jnp.bfloat16)
         to_partner(level, tile).start()
@@ -279,25 +274,20 @@
             columns = slice(tile * TILE, tile * TILE + TILE)
             to_partner(level, tile).wait_recv()
 
-            def theirs(step, carry, level=level, tile=tile, columns=columns):
-                rows = pl.ds(pl.multiple_of(step * TILE, TILE), TILE)
-                low_rows = pl.ds(pl.multiple_of(step * TILE + ANGLES, TILE), TILE)
-                matrix = chosen[level, 1, rows, :]
-                real = jnp.dot(matrix, taken[level, tile, 0], preferred_element_type=jnp.float32)
-                imag = jnp.dot(matrix, taken[level, tile, 1], preferred_element_type=jnp.float32)
-                cosine = cos_table[level, 1, rows, columns]
-                sine = sin_table[level, 1, rows, columns]
-                high = total[rows, columns] + (real * cosine - imag * sine)
-                low = total[low_rows, columns] + (real * sine + imag * cosine)
-                if level + 1 < LEVELS:
-                    images[level + 1, rows, columns] = high.astype(jnp.bfloat16)
-                    images[level + 1, low_rows, columns] = low.astype(jnp.bfloat16)
-                else:
-                    total[rows, columns] = high
-                    total[low_rows, columns] = low
-                return carry
-
-            lax.fori_loop(0, ANGLES // TILE, theirs, 0)
+            matrix = chosen[level, 1]
+            real = jnp.dot(matrix, taken[level, tile, 0], preferred_element_type=jnp.float32)
+            imag = jnp.dot(matrix, taken[level, tile, 1], preferred_element_type=jnp.float32)
+            cosine = cos_table[level, 1, :, columns]
+            sine = sin_table[level, 1, :, columns]
+            high = total[0:ANGLES, columns] + (real * cosine - imag * sine)
+            low = total[ANGLES : 2 * ANGLES, columns] + (real * sine + imag * cosine)
+            if level + 1 < LEVELS:
+                images[level + 1, 0:ANGLES, columns] = high.astype(jnp.bfloat16)
+                images[level + 1, ANGLES : 2 * ANGLES, columns] = low.astype(jnp.bfloat16)
+            else:
+                total[0:ANGLES, columns] = high
+                total[ANGLES : 2 * ANGLES, columns] = low
+
             if level + 1 < LEVELS:
                 send_rims(level + 1, left=tile == 0, right=tile == TILES - 1)
                 if order == 2:

time: 148 us -> 142 us (0.959)
  the two profiles are of different devices: /device:TPU:128 before, /device:TPU:39 now
where the time goes in v4:
time: 142 us
  Pallas kernels  139 us (98%)
  local copies, waits for them, and re-layouts  3.08 us (2%)
    pallas_call x1, Pallas kernels, on_device(): pl.pallas_call(functools.partial(kernel, sources, total_bins), out_shape=...  139 us
    unnamed x1, local copies, waits for them, and re-layouts  3.08 us

profile of v4, /device:TPU:39, one launch (start us, length us, event | category | flops | bytes accessed | tf_op | source)
XLA Modules:
  0.0 141.7 jit_solution(14925765082554818232)
XLA Ops:
  0.0 138.6 %shard_map.73 = f32[2,512,512]{2,1,0:T(8,128)} custom-call(bf16[16,32768]{1,0:T(8,128)(2,1)} %bitcast.3, bf16[1024,1024]{1,0:T(8,128)(2,1)} %constant.2.clone.doppler, bf16[3,544,512]{2,1,0:T(8,128)(2,1)} %kernels_far.1, bf16[3,2,512,256]{3,2,1,0:T(8,128)(2,1)} %interp_far.1, s32[3,1,8]{2,1,0:T(1,128)} %bitcast.4, s32[3,1,8]{2,1,0:T(1,128)} %bitcast.5, ...), custom_call_target="tpu_custom_call" | custom-call | tf_op jit(solution)/shard_map/pallas_call | solution.py:326
  138.6 3.1 %copy.9 = f32[2,512,512]{2,1,0:T(8,128)} copy(f32[2,512,512]{2,1,0:T(8,128)} %shard_map.73) | data formatting | bytes 4194304

commit v5 on v4

--- a/solution.py
+++ b/solution.py
@@ -256,19 +256,15 @@
     for tile in ORDERS[0]:
         resample(0, tile)
     for level in range(LEVELS):
-        def own(step, carry, level=level):
-            rows = pl.ds(pl.multiple_of(step * TILE, TILE), TILE)
-            low_rows = pl.ds(pl.multiple_of(step * TILE + ANGLES, TILE), TILE)
-            matrix = chosen[level, 0, rows, :]
-            real = jnp.dot(matrix, kept[0], preferred_element_type=jnp.float32)
-            imag = jnp.dot(matrix, kept[1], preferred_element_type=jnp.float32)
-            cosine = cos_table[level, 0, rows, :]
-            sine = sin_table[level, 0, rows, :]
-            total[rows, :] = real * cosine - imag * sine
-            total[low_rows, :] = real * sine + imag * cosine
-            return carry
-
-        lax.fori_loop(0, ANGLES // TILE, own, 0)
+        for tile in ORDERS[level]:
+            columns = slice(tile * TILE, tile * TILE + TILE)
+            matrix = chosen[level, 0]
+            real = jnp.dot(matrix, kept[0, :, columns], preferred_element_type=jnp.float32)
+            imag = jnp.dot(matrix, kept[1, :, columns], preferred_element_type=jnp.float32)
+            cosine = cos_table[level, 0, :, columns]
+            sine = sin_table[level, 0, :, columns]
+            total[0:ANGLES, columns] = real * cosine - imag * sine
+            total[ANGLES : 2 * ANGLES, columns] = real * sine + imag * cosine
 
         for order, tile in enumerate(ORDERS[level]):
             columns = slice(tile * TILE, tile * TILE + TILE)

time: 142 us -> 141 us (level)
  no operation moved by 1% of the time
where the time goes in v5:
time: 141 us
  Pallas kernels  138 us (98%)
  local copies, waits for them, and re-layouts  3.08 us (2%)
    pallas_call x1, Pallas kernels, on_device(): pl.pallas_call(functools.partial(kernel, sources, total_bins), out_shape=...  138 us
    unnamed x1, local copies, waits for them, and re-layouts  3.08 us

profile of v5, /device:TPU:39, one launch (start us, length us, event | category | flops | bytes accessed | tf_op | source)
XLA Modules:
  0.0 140.7 jit_solution(9367271798176328723)
XLA Ops:
  0.0 137.6 %shard_map.73 = f32[2,512,512]{2,1,0:T(8,128)} custom-call(bf16[16,32768]{1,0:T(8,128)(2,1)} %bitcast.3, bf16[1024,1024]{1,0:T(8,128)(2,1)} %constant.2.clone.doppler, bf16[3,544,512]{2,1,0:T(8,128)(2,1)} %kernels_far.1, bf16[3,2,512,256]{3,2,1,0:T(8,128)(2,1)} %interp_far.1, s32[3,1,8]{2,1,0:T(1,128)} %bitcast.4, s32[3,1,8]{2,1,0:T(1,128)} %bitcast.5, ...), custom_call_target="tpu_custom_call" | custom-call | tf_op jit(solution)/shard_map/pallas_call | solution.py:322
  137.6 3.1 %copy.9 = f32[2,512,512]{2,1,0:T(8,128)} copy(f32[2,512,512]{2,1,0:T(8,128)} %shard_map.73) | data formatting | bytes 4194304
